TPU v7x, 32 devices: a whole 2x2x4 slice. The times are simulated.
32 devices in a mesh: section: 4 (over x, core), ctx: 8 (over z, y).
Axes of the slice: x: 2, y: 2, z: 4, core: 2. Of those that a mesh axis runs over, the one named last changes fastest.
Arguments:
- block_order: int32 [8], replicated, may hold values from 0 to 7, each once
- queries: bfloat16 [4, 64, 2560], P('section', 'ctx'), may hold values from -400 to 400
- cache_keys: bfloat16 [1024, 2560], P('ctx', 'section'), may hold values from -6 to 6
- cache_values: bfloat16 [1024, 2560], P('ctx', 'section'), may hold values from -6 to 6
- attention_out: bfloat16 [4, 64, 2560], P('section', 'ctx'), may hold values from -6 to 6
- output_grad: bfloat16 [4, 64, 2560], P('section', 'ctx'), may hold values from -192 to 192
Outputs:
- grad_queries: bfloat16 [4, 64, 2560], P('section', 'ctx')
- grad_keys: bfloat16 [1024, 2560], P('ctx', 'section')
- grad_values: bfloat16 [1024, 2560], P('ctx', 'section')
Inputs may be any that keep to these rules, and one draw needn't show every extreme that they name: `block_order`: every block number once.
All inputs are finite; a program needn't handle non-finite values.
Results may differ from a plain program's by a relative error of at most 0.012.
Values may be sent and summed in bfloat16 or wider, within the bound.
No kernel may reach another device: no remote copies, remote signals or barrier semaphores. Data moves between devices by JAX's collectives and lax.ppermute only.
A program may use at most 64 MiB of HBM per device.

v0:
```python
import jax
import jax.numpy as jnp
from jax import lax
from jax.sharding import PartitionSpec as P

HEADS = 20
HEAD_DIM = 128
masked_score = -1e30


def local(block_order, queries, cache_keys, cache_values, attention_out, output_grad):
    ctx_count = lax.axis_size("ctx")
    rows_here = queries.shape[1]
    key_count = cache_keys.shape[0]
    key_total = key_count * ctx_count
    query_count = rows_here * ctx_count
    scaling = HEAD_DIM ** (-0.5)
    product = output_grad.astype(jnp.float32) * attention_out.astype(jnp.float32)
    delta_terms = jnp.sum(product.reshape(1, rows_here, HEADS, HEAD_DIM), axis=3)
    query_part, grad_part, delta_part = (queries, output_grad, delta_terms)
    key_block, value_block = (
        lax.all_gather(cache_keys, "section", axis=1, tiled=True),
        lax.all_gather(cache_values, "section", axis=1, tiled=True),
    )
    group_heads = HEADS
    layers = query_part.shape[0]
    pair_count = layers * group_heads
    query_all, grad_all = (
        lax.all_gather(query_part, "ctx", axis=1, tiled=True),
        lax.all_gather(grad_part, "ctx", axis=1, tiled=True),
    )
    delta_all = lax.all_gather(delta_part, "ctx", axis=1, tiled=True)

    def split_heads(values):
        return (
            values.reshape(layers, query_count, group_heads, HEAD_DIM)
            .transpose(0, 2, 1, 3)
            .reshape(pair_count, query_count, HEAD_DIM)
        )

    query_heads = split_heads(query_all)
    grad_heads = split_heads(grad_all)
    delta_heads = delta_all.transpose(0, 2, 1).reshape(pair_count, query_count)
    key_heads = key_block.reshape(key_count, group_heads, HEAD_DIM).transpose(1, 0, 2)
    value_heads = value_block.reshape(key_count, group_heads, HEAD_DIM).transpose(1, 0, 2)
    head_ids = jnp.arange(pair_count, dtype=jnp.int32) % group_heads
    ctx_index = lax.axis_index("ctx")
    key_pos = block_order[ctx_index] * key_count + jnp.arange(key_count, dtype=jnp.int32)
    query_pos = key_total - query_count + jnp.arange(query_count, dtype=jnp.int32)
    visible = key_pos[None, :] <= query_pos[:, None]

    def masked_scores(query_head, head_index):
        scores = (
            jnp.dot(query_head, key_heads[head_index].T, preferred_element_type=jnp.float32)
            * scaling
        )
        return jnp.where(visible, scores, masked_score)

    def local_stats(packed):
        query_head, head_index = packed
        scores = masked_scores(query_head, head_index)
        row_max = jnp.max(scores, axis=1)
        row_sum = jnp.sum(jnp.where(visible, jnp.exp(scores - row_max[:, None]), 0.0), axis=1)
        return (row_max, row_sum)

    row_max, row_sum = lax.map(local_stats, (query_heads, head_ids))
    peak_max = lax.pmax(row_max.astype(jnp.bfloat16), "ctx").astype(row_max.dtype)
    row_sum = lax.psum(row_sum * jnp.exp(row_max - peak_max), "ctx")
    row_max = peak_max
    log_total = row_max + jnp.log(row_sum)

    def gradients(packed):
        query_head, grad_head, delta_head, total_head, head_index = packed
        scores = masked_scores(query_head, head_index)
        prob = jnp.where(visible, jnp.exp(scores - total_head[:, None]), 0.0)
        prob_b = prob.astype(jnp.bfloat16)
        value_grad = jnp.dot(prob_b.T, grad_head, preferred_element_type=jnp.float32)
        prob_grad = jnp.dot(
            grad_head, value_heads[head_index].T, preferred_element_type=jnp.float32
        )
        score_grad = (prob * (prob_grad - delta_head[:, None]) * scaling).astype(jnp.bfloat16)
        query_grad = jnp.dot(score_grad, key_heads[head_index], preferred_element_type=jnp.float32)
        key_grad = jnp.dot(score_grad.T, query_head, preferred_element_type=jnp.float32)
        return (query_grad, key_grad, value_grad)

    query_grad, key_grad, value_grad = lax.map(
        gradients, (query_heads, grad_heads, delta_heads, log_total, head_ids)
    )
    query_layout = (
        query_grad.reshape(layers, group_heads, query_count, HEAD_DIM)
        .transpose(0, 2, 1, 3)
        .reshape(layers, query_count, group_heads * HEAD_DIM)
    )
    query_rows_sum = lax.psum_scatter(query_layout, "ctx", scatter_dimension=1, tiled=True)
    key_sum = (
        key_grad.reshape(layers, group_heads, key_count, HEAD_DIM)
        .sum(axis=0)
        .transpose(1, 0, 2)
        .reshape(key_count, group_heads * HEAD_DIM)
    )
    value_sum = (
        value_grad.reshape(layers, group_heads, key_count, HEAD_DIM)
        .sum(axis=0)
        .transpose(1, 0, 2)
        .reshape(key_count, group_heads * HEAD_DIM)
    )
    grad_queries = query_rows_sum.astype(jnp.bfloat16)
    key_part, value_part = (
        lax.psum_scatter(
            key_sum.astype(jnp.bfloat16), "section", scatter_dimension=1, tiled=True
        ).astype(jnp.float32),
        lax.psum_scatter(
            value_sum.astype(jnp.bfloat16), "section", scatter_dimension=1, tiled=True
        ).astype(jnp.float32),
    )
    grad_keys = key_part.astype(jnp.bfloat16)
    grad_values = value_part.astype(jnp.bfloat16)
    return (grad_queries, grad_keys, grad_values)


def solution(mesh):
    in_specs = (
        P(),
        P("section", "ctx", None),
        P("ctx", "section"),
        P("ctx", "section"),
        P("section", "ctx", None),
        P("section", "ctx", None),
    )
    out_specs = (P("section", "ctx", None), P("ctx", "section"), P("ctx", "section"))
    return jax.shard_map(local, mesh=mesh, in_specs=in_specs, out_specs=out_specs, check_vma=False)
```

profile of v0, /device:TPU:0, one launch (start us, length us, event | category | flops | bytes accessed | tf_op | source)
XLA Modules:
  0.0 449.6 jit_solution(16274756989076429292)
XLA Ops:
  9.2 33.0 %all_gather.17 = bf16[1,64,2560]{2,1,0:T(8,128)(2,1)S(1)} all-gather(bf16[1,8,2560]{2,1,0:T(8,128)(2,1)} %param.15), channel_id=1, replica_groups=mesh['section'=4,'ctx'=8] {'ctx'}, dimensions={1}, use_global_device_ids=true | all-gather | bytes 368640 | tf_op jit(solution)/shard_map/all_gather | solution.py:30
  42.4 30.6 %all-gather = f32[64,20]{1,0:T(8,128)S(1)} all-gather(f32[8,20]{1,0:T(8,128)S(1)} %copy.43), channel_id=2, replica_groups=mesh['section'=4,'ctx'=8] {'ctx'}, dimensions={0}, use_global_device_ids=true | all-gather | bytes 5760 | tf_op jit(solution)/shard_map/all_gather | solution.py:32
  74.8 30.8 %all_gather.15 = bf16[1,64,2560]{2,1,0:T(8,128)(2,1)S(1)} all-gather(bf16[1,8,2560]{2,1,0:T(8,128)(2,1)S(1)} %copy-done.4), channel_id=1, replica_groups=mesh['section'=4,'ctx'=8] {'ctx'}, dimensions={1}, use_global_device_ids=true | all-gather | bytes 368640 | tf_op jit(solution)/shard_map/all_gather | solution.py:29
  106.2 7.9 %all_gather.18 = bf16[128,2560]{0,1:T(8,128)(2,1)S(1)} all-gather(bf16[128,640]{0,1:T(8,128)(2,1)S(1)} %copy.42), channel_id=1, replica_groups=mesh['section'=4,'ctx'=8] {'section'}, dimensions={1}, use_global_device_ids=true | all-gather | bytes 819200 | tf_op jit(solution)/shard_map/all_gather | solution.py:23
  114.1 8.0 %all_gather.16 = bf16[128,2560]{0,1:T(8,128)(2,1)S(1)} all-gather(bf16[128,640]{0,1:T(8,128)(2,1)S(1)} %copy.39), channel_id=1, replica_groups=mesh['section'=4,'ctx'=8] {'section'}, dimensions={1}, use_global_device_ids=true | all-gather | bytes 819200 | tf_op jit(solution)/shard_map/all_gather | solution.py:22
  122.4 61.5 %while.28 = (s32[]{:T(128)}, f32[20,64]{1,0:T(8,128)S(1)}, f32[20,64]{1,0:T(8,128)S(1)}, bf16[20,64,128]{2,1,0:T(8,128)(2,1)S(1)}, s32[20]{0:T(128)S(1)}, /*inde...) while((s32[]{:T(128)}, f32[20,64]{1,0:T(8,128)S(1)}, ...), condition=%wide.region_4.5_spmd.clone, body=%wide.region_1.4_spmd.clone.sunk | while | flops 2162565 | bytes 118451 | solution.py:66
  184.0 21.7 %pmax.7 = bf16[20,64]{1,0:T(8,128)(2,1)S(1)} all-reduce(bf16[20,64]{1,0:T(8,128)(2,1)S(1)} %convert_element_type.43), channel_id=1, replica_groups=mesh['section'=4,'ctx'=8] {'ctx'}, use_global_device_ids=true, to_apply=%region_5.6 | all-reduce | flops 1280 | bytes 5120 | tf_op jit(solution)/shard_map/pmax | solution.py:67
  205.7 33.0 %psum.7 = f32[20,64]{1,0:T(8,128)S(1)} all-reduce(f32[20,64]{1,0:T(8,128)S(1)} %fusion.44), channel_id=1, replica_groups=mesh['section'=4,'ctx'=8] {'ctx'}, use_global_device_ids=true, to_apply=%region_6.7 | all-reduce | flops 1280 | bytes 10240 | tf_op jit(solution)/shard_map/psum | solution.py:68
  238.7 92.9 %while.29 = (s32[]{:T(128)}, f32[20,64,128]{2,1,0:T(8,128)S(1)}, bf16[20,128,128]{1,2,0:T(8,128)(2,1)}, bf16[20,128,128]{1,2,0:T(8,128)(2,1)}, bf16[20,64,128]{2...) while((s32[]{:T(128)}, f32[20,64,128]{2,1,0:T(8,128)S(1)}, ...), condition=%wide.region_8.9_spmd.clone, body=%wide.region_7.8_spmd.clone.sunk | while | flops 10567685 | bytes 480487 | solution.py:86
  255.4 0.9 fusion.84
  264.7 0.9 fusion.84
  274.0 0.9 fusion.84
  287.9 0.9 fusion.84
  292.6 0.9 fusion.84
  301.9 0.9 fusion.84
  311.2 0.9 fusion.84
  329.7 0.9 fusion.84
  332.4 0.9 copy_bitcast_fusion
  333.3 17.2 %reduce-scatter.8.cloned.1.call-done = bf16[128,640]{0,1:T(8,128)(2,1)} async-done(((bf16[128,2560]{0,1:T(8,128)(2,1)}), bf16[128,640]{0,1:T(8,128)(2,1)}) %reduce-scatter.8.cloned.1.call-update) | async-done | bytes 163856 | tf_op jit(solution)/shard_map/reduce_scatter | solution.py:112
  350.5 1.7 copy.53
  352.2 23.3 %reduce-scatter.6.cloned.1.call-done = bf16[128,640]{0,1:T(8,128)(2,1)} async-done(((bf16[128,2560]{0,1:T(8,128)(2,1)}), bf16[128,640]{0,1:T(8,128)(2,1)}) %reduce-scatter.6.cloned.1.call-update) | async-done | bytes 163856 | tf_op jit(solution)/shard_map/reduce_scatter | solution.py:109
  375.5 1.7 copy.52
  377.2 64.4 %reduce-scatter.4.cloned.1.call-done = f32[1,8,2560]{2,1,0:T(8,128)} async-done(((f32[1,64,2560]{2,1,0:T(8,128)}), f32[1,8,2560]{2,1,0:T(8,128)}) %reduce-scatter.4.cloned.1.call-update) | async-done | bytes 81936 | tf_op jit(solution)/shard_map/reduce_scatter | solution.py:94
  441.6 1.5 convert_element_type.47
  (273 shorter events, 73.8 us)
Async XLA Ops:
  7.2 343.3 %reduce-scatter.8.cloned.1.call-start = ((), (), s32[]{:S(2)}) async-start(), calls=%async_computation.5 | async-start | bytes 819200 | tf_op jit(solution)/shard_map/reduce_scatter | solution.py:112
  7.3 0.7 copy-start.5
  9.2 33.0 %copy-start.2 = (bf16[1,8,2560]{2,1,0:T(8,128)(2,1)S(1)}, bf16[1,8,2560]{2,1,0:T(8,128)(2,1)}, u32[]{:S(2)}) copy-start(bf16[1,8,2560]{2,1,0:T(8,128)(2,1)} %param.15) | copy-start | bytes 122884
  9.2 33.0 %copy-start.3 = (bf16[1,8,2560]{2,1,0:T(8,128)(2,1)S(1)}, bf16[1,8,2560]{2,1,0:T(8,128)(2,1)}, u32[]{:S(2)}) copy-start(bf16[1,8,2560]{2,1,0:T(8,128)(2,1)} %param.14) | copy-start | bytes 122884
  42.2 30.9 %copy-start = (bf16[128,640]{1,0:T(8,128)(2,1)S(1)}, bf16[128,640]{1,0:T(8,128)(2,1)}, u32[]{:S(2)}) copy-start(bf16[128,640]{1,0:T(8,128)(2,1)} %param.12) | copy-start | bytes 491524
  73.1 0.9 copy-start.1
  74.0 0.8 copy-start.4
  331.6 43.9 %reduce-scatter.6.cloned.1.call-start = ((), (), s32[]{:S(2)}) async-start(), calls=%async_computation.4 | async-start | bytes 819200 | tf_op jit(solution)/shard_map/reduce_scatter | solution.py:109
  332.4 109.2 %reduce-scatter.4.cloned.1.call-start = ((), (), s32[]{:S(2)}) async-start(), calls=%async_computation.3 | async-start | bytes 737280 | tf_op jit(solution)/shard_map/reduce_scatter | solution.py:94
Sparse Core Ops, SparseCore 0:
  331.7 18.7 reduce-scatter.7
  353.0 22.4 reduce-scatter.5
  378.8 62.7 reduce-scatter.3
where the time goes:
time: 451 us; the launch traced here: 450 us
  blocking collectives  165 us (37%)
  waiting for transfers between devices  106 us (24%)
  loops' own time  78.6 us (17%)
  matrix products  46.9 us (10%)
  local copies, waits for them, and re-layouts  33.4 us (7%)
  between operations  14.6 us (3%)
  other arithmetic  5.47 us (1%)
    reduce_scatter x1, waiting for transfers between devices, local(): lax.psum_scatter(query_layout, 'ctx', scatter_dimension=1, tiled=True)  64.4 us
    another operation x1, loops' own time, local(): row_max, row_sum = lax.map(local_stats, (query_heads, head_ids))  39.3 us
    another operation x1, loops' own time, local(): lax.map(gradients, (query_heads, grad_heads, delta_heads, log_total, head...  39.3 us
    all_gather x1, blocking collectives, local(): lax.all_gather(grad_part, 'ctx', axis=1, tiled=True)  33 us
    psum x1, blocking collectives, local(): row_sum = lax.psum(row_sum * jnp.exp(row_max - peak_max), 'ctx')  33 us
    all_gather x1, blocking collectives, local(): lax.all_gather(query_part, 'ctx', axis=1, tiled=True)  30.8 us
    all_gather x1, blocking collectives, local(): delta_all = lax.all_gather(delta_part, 'ctx', axis=1, tiled=True)  30.6 us
    dynamic_slice x40, local copies, waits for them, and re-layouts, local(): row_max, row_sum = lax.map(local_stats, (query_heads, head_ids))  23.4 us
  transfers between devices with their start and end apart: 3, of which 3 were waited for; matrix products, arithmetic and copies ran while one was open for 1% of the time, Pallas kernels for 0%

commit v1 on v0

--- a/solution.py
+++ b/solution.py
@@ -6,6 +6,18 @@
 HEADS = 20
 HEAD_DIM = 128
 masked_score = -1e30
+
+
+def doubled_up(x, axis, dim):
+    ways, here = (lax.axis_size(axis), lax.axis_index(axis))
+    grown, reach = (x, 1)
+    while reach < ways:
+        theirs = lax.ppermute(grown, axis, [(d, d ^ reach) for d in range(ways)])
+        mine_first = jnp.concatenate([grown, theirs], axis=dim)
+        theirs_first = jnp.concatenate([theirs, grown], axis=dim)
+        grown = jnp.where(here & reach == 0, mine_first, theirs_first)
+        reach = 2 * reach
+    return grown
 
 
 def local(block_order, queries, cache_keys, cache_values, attention_out, output_grad):
@@ -27,7 +39,7 @@
     pair_count = layers * group_heads
     query_all, grad_all = (
         lax.all_gather(query_part, "ctx", axis=1, tiled=True),
-        lax.all_gather(grad_part, "ctx", axis=1, tiled=True),
+        doubled_up(grad_part, "ctx", 1),
     )
     delta_all = lax.all_gather(delta_part, "ctx", axis=1, tiled=True)
 

time: 451 us -> 433 us (0.960)
  blocking collectives: 165 us -> 131 us
  waiting for transfers between devices: 106 us -> 118 us
    all_gather x1 -> x0, blocking collectives: 33 us -> none  [local(): lax.all_gather(grad_part, 'ctx', axis=1, tiled=True)]
    ppermute x0 -> x3, waiting for transfers between devices: none -> 11.6 us  [doubled_up(): theirs = lax.ppermute(grown, axis, [(d, d ^ reach) for d in range(ways)])]
  transfers between devices with their start and end apart: 3 -> 6, of which waited for: 3 -> 5; matrix products, arithmetic and copies ran while one was open for 1% -> 7% of each run, Pallas kernels for 0% -> 0%
where the time goes in v1:
time: 433 us; the launch traced here: 432 us
  blocking collectives  131 us (30%)
  waiting for transfers between devices  118 us (27%)
  loops' own time  78.6 us (18%)
  matrix products  46.9 us (11%)
  local copies, waits for them, and re-layouts  33.5 us (8%)
  between operations  14.6 us (3%)
  other arithmetic  5.7 us (1%)
    reduce_scatter x1, waiting for transfers between devices, local(): lax.psum_scatter(query_layout, 'ctx', scatter_dimension=1, tiled=True)  64.3 us
    another operation x1, loops' own time, local(): row_max, row_sum = lax.map(local_stats, (query_heads, head_ids))  39.3 us
    another operation x1, loops' own time, local(): lax.map(gradients, (query_heads, grad_heads, delta_heads, log_total, head...  39.3 us
    psum x1, blocking collectives, local(): row_sum = lax.psum(row_sum * jnp.exp(row_max - peak_max), 'ctx')  33 us
    all_gather x1, blocking collectives, local(): lax.all_gather(query_part, 'ctx', axis=1, tiled=True)  31.4 us
    all_gather x1, blocking collectives, local(): delta_all = lax.all_gather(delta_part, 'ctx', axis=1, tiled=True)  30.6 us
    dynamic_slice x40, local copies, waits for them, and re-layouts, local(): row_max, row_sum = lax.map(local_stats, (query_heads, head_ids))  23.4 us
    reduce_scatter x1, waiting for transfers between devices, local(): lax.psum_scatter(key_sum.astype(jnp.bfloat16), 'section', scatter_dimensi...  23.3 us
  transfers between devices with their start and end apart: 6, of which 5 were waited for; matrix products, arithmetic and copies ran while one was open for 7% of the time, Pallas kernels for 0%

profile of v1, /device:TPU:0, one launch (start us, length us, event | category | flops | bytes accessed | tf_op | source)
XLA Modules:
  0.0 431.8 jit_solution(29764947101411643)
XLA Ops:
  7.2 3.1 collective-permute-start
  12.2 1.1 copy.58
  14.1 31.4 %all_gather.12 = bf16[1,64,2560]{2,1,0:T(8,128)(2,1)S(1)} all-gather(bf16[1,8,2560]{2,1,0:T(8,128)(2,1)S(1)} %copy-done.3), channel_id=1, replica_groups=mesh['section'=4,'ctx'=8] {'ctx'}, dimensions={1}, use_global_device_ids=true | all-gather | bytes 368640 | tf_op jit(solution)/shard_map/all_gather | solution.py:41
  45.8 7.9 %all_gather.14 = bf16[128,2560]{0,1:T(8,128)(2,1)S(1)} all-gather(bf16[128,640]{0,1:T(8,128)(2,1)S(1)} %copy.65), channel_id=1, replica_groups=mesh['section'=4,'ctx'=8] {'section'}, dimensions={1}, use_global_device_ids=true | all-gather | bytes 819200 | tf_op jit(solution)/shard_map/all_gather | solution.py:35
  53.7 8.0 %all_gather.13 = bf16[128,2560]{0,1:T(8,128)(2,1)S(1)} all-gather(bf16[128,640]{0,1:T(8,128)(2,1)S(1)} %copy.58), channel_id=1, replica_groups=mesh['section'=4,'ctx'=8] {'section'}, dimensions={1}, use_global_device_ids=true | all-gather | bytes 819200 | tf_op jit(solution)/shard_map/all_gather | solution.py:34
  62.0 61.5 %while.28 = (s32[]{:T(128)}, f32[20,64]{1,0:T(8,128)S(1)}, f32[20,64]{1,0:T(8,128)S(1)}, bf16[20,64,128]{2,1,0:T(8,128)(2,1)S(1)}, s32[20]{0:T(128)S(1)}, /*inde...) while((s32[]{:T(128)}, f32[20,64]{1,0:T(8,128)S(1)}, ...), condition=%wide.region_4.5_spmd.clone, body=%wide.region_1.4_spmd.clone.sunk | while | flops 2162565 | bytes 118451 | solution.py:78
  123.5 20.6 %pmax.7 = bf16[20,64]{1,0:T(8,128)(2,1)S(1)} all-reduce(bf16[20,64]{1,0:T(8,128)(2,1)S(1)} %convert_element_type.43), channel_id=1, replica_groups=mesh['section'=4,'ctx'=8] {'ctx'}, use_global_device_ids=true, to_apply=%region_5.6 | all-reduce | flops 1280 | bytes 5120 | tf_op jit(solution)/shard_map/pmax | solution.py:79
  144.2 33.0 %psum.7 = f32[20,64]{1,0:T(8,128)S(1)} all-reduce(f32[20,64]{1,0:T(8,128)S(1)} %fusion.47), channel_id=1, replica_groups=mesh['section'=4,'ctx'=8] {'ctx'}, use_global_device_ids=true, to_apply=%region_6.7 | all-reduce | flops 1280 | bytes 10240 | tf_op jit(solution)/shard_map/psum | solution.py:80
  177.5 30.6 %all-gather = f32[64,20]{1,0:T(8,128)S(1)} all-gather(f32[8,20]{1,0:T(8,128)S(1)} %copy.66), channel_id=2, replica_groups=mesh['section'=4,'ctx'=8] {'ctx'}, dimensions={0}, use_global_device_ids=true | all-gather | bytes 5760 | tf_op jit(solution)/shard_map/all_gather | solution.py:44
  208.3 4.4 %collective-permute-done.1 = bf16[1,16,2560]{2,1,0:T(8,128)(2,1)S(1)} collective-permute-done((bf16[1,16,2560]{2,1,0:T(8,128)(2,1)S(1)}, bf16[1,16,2560]{2,1,0:T(8,128)(2,1)S(1)}, u32[]{:S(2)}, u32[]{:S(2)}) %collective-permute-start.1) | collective-permute-done | bytes 81952 | tf_op jit(solution)/shard_map/ppermute | solution.py:15
  213.0 7.2 %collective-permute-done.2 = bf16[1,32,2560]{2,1,0:T(8,128)(2,1)S(1)} collective-permute-done((bf16[1,32,2560]{2,1,0:T(8,128)(2,1)S(1)}, bf16[1,32,2560]{2,1,0:T(8,128)(2,1)S(1)}, u32[]{:S(2)}, u32[]{:S(2)}) %collective-permute-start.2) | collective-permute-done | bytes 163872 | tf_op jit(solution)/shard_map/ppermute | solution.py:15
  220.3 92.9 %while.29 = (s32[]{:T(128)}, f32[20,64,128]{2,1,0:T(8,128)S(1)}, bf16[20,128,128]{1,2,0:T(8,128)(2,1)}, bf16[20,128,128]{1,2,0:T(8,128)(2,1)}, bf16[20,64,128]{2...) while((s32[]{:T(128)}, f32[20,64,128]{2,1,0:T(8,128)S(1)}, ...), condition=%wide.region_8.9_spmd.clone, body=%wide.region_7.8_spmd.clone.sunk | while | flops 10567685 | bytes 480487 | solution.py:98
  237.1 0.9 fusion.88
  246.4 0.9 fusion.88
  274.2 0.9 fusion.88
  292.8 0.9 fusion.88
  311.4 0.9 fusion.88
  314.0 0.9 copy_bitcast_fusion
  314.9 17.8 %reduce-scatter.8.cloned.1.call-done = bf16[128,640]{0,1:T(8,128)(2,1)} async-done(((bf16[128,2560]{0,1:T(8,128)(2,1)}), bf16[128,640]{0,1:T(8,128)(2,1)}) %reduce-scatter.8.cloned.1.call-update) | async-done | bytes 163856 | tf_op jit(solution)/shard_map/reduce_scatter | solution.py:124
  332.7 1.7 copy.75
  334.4 23.3 %reduce-scatter.6.cloned.1.call-done = bf16[128,640]{0,1:T(8,128)(2,1)} async-done(((bf16[128,2560]{0,1:T(8,128)(2,1)}), bf16[128,640]{0,1:T(8,128)(2,1)}) %reduce-scatter.6.cloned.1.call-update) | async-done | bytes 163856 | tf_op jit(solution)/shard_map/reduce_scatter | solution.py:121
  357.7 1.7 copy.74
  359.4 64.3 %reduce-scatter.4.cloned.1.call-done = f32[1,8,2560]{2,1,0:T(8,128)} async-done(((f32[1,64,2560]{2,1,0:T(8,128)}), f32[1,8,2560]{2,1,0:T(8,128)}) %reduce-scatter.4.cloned.1.call-update) | async-done | bytes 81936 | tf_op jit(solution)/shard_map/reduce_scatter | solution.py:106
  423.8 1.5 convert_element_type.47
  (283 shorter events, 75.7 us)
Async XLA Ops:
  7.2 325.6 %reduce-scatter.8.cloned.1.call-start = ((), (), s32[]{:S(2)}) async-start(), calls=%async_computation.5 | async-start | bytes 819200 | tf_op jit(solution)/shard_map/reduce_scatter | solution.py:124
  7.2 200.9 %collective-permute-start = (bf16[1,8,2560]{2,1,0:T(8,128)(2,1)}, bf16[1,8,2560]{2,1,0:T(8,128)(2,1)S(1)}, u32[]{:S(2)}, u32[]{:S(2)}) collective-permute-start(bf16[1,8,2560]{2,1,0:T(8,128)(2,1)} %param.15), channel_id=1, source_target_pairs={{0,1},{1,0},{2,3},{3,2},{4,5},{5,4},{6,7},{7,6},{8,9},{9,8},{10,11... | collective-permute-start | bytes 122888 | tf_op jit(solution)/shard_map/ppermute | solution.py:15
  10.3 0.7 copy-start.4
  12.2 1.1 copy-start.1
  13.3 0.8 copy-start.3
  144.2 33.0 %copy-start = (bf16[1,8,2560]{2,1,0:T(8,128)(2,1)S(1)}, bf16[1,8,2560]{2,1,0:T(8,128)(2,1)}, u32[]{:S(2)}) copy-start(bf16[1,8,2560]{2,1,0:T(8,128)(2,1)} %param.15) | copy-start | bytes 122884
  144.2 33.0 %copy-start.2 = (bf16[1,8,2560]{2,1,0:T(8,128)(2,1)S(1)}, bf16[1,8,2560]{2,1,0:T(8,128)(2,1)}, u32[]{:S(2)}) copy-start(bf16[1,8,2560]{2,1,0:T(8,128)(2,1)} %param.14) | copy-start | bytes 122884
  208.2 4.5 %collective-permute-start.1 = (bf16[1,16,2560]{2,1,0:T(8,128)(2,1)S(1)}, bf16[1,16,2560]{2,1,0:T(8,128)(2,1)S(1)}, u32[]{:S(2)}, u32[]{:S(2)}) collective-permute-start(bf16[1,16,2560]{2,1,0:T(8,128)(2,1)S(1)} %maximum_select_fusion.4), channel_id=1, source_target_pairs={{0,2},{1,3},{2,0},{3,1},{4,6},{5,7},{6,4},{7,5},{8,10},{9,11},{10,... | collective-permute-start | bytes 245768 | tf_op jit(solution)/shard_map/ppermute | solution.py:15
  212.7 7.5 %collective-permute-start.2 = (bf16[1,32,2560]{2,1,0:T(8,128)(2,1)S(1)}, bf16[1,32,2560]{2,1,0:T(8,128)(2,1)S(1)}, u32[]{:S(2)}, u32[]{:S(2)}) collective-permute-start(bf16[1,32,2560]{2,1,0:T(8,128)(2,1)S(1)} %maximum_select_fusion.2), channel_id=1, source_target_pairs={{0,4},{1,5},{2,6},{3,7},{4,0},{5,1},{6,2},{7,3},{8,12},{9,13},{10,... | collective-permute-start | bytes 491528 | tf_op jit(solution)/shard_map/ppermute | solution.py:15
  313.2 44.5 %reduce-scatter.6.cloned.1.call-start = ((), (), s32[]{:S(2)}) async-start(), calls=%async_computation.4 | async-start | bytes 819200 | tf_op jit(solution)/shard_map/reduce_scatter | solution.py:121
  314.0 109.8 %reduce-scatter.4.cloned.1.call-start = ((), (), s32[]{:S(2)}) async-start(), calls=%async_computation.3 | async-start | bytes 737280 | tf_op jit(solution)/shard_map/reduce_scatter | solution.py:106
Sparse Core Ops, SparseCore 0:
  313.4 19.3 reduce-scatter.7
  335.2 22.4 reduce-scatter.5
  361.0 62.7 reduce-scatter.3
